TPU v7x, 32 devices: a whole 2x2x4 slice. The times are simulated.
32 devices in a mesh: row: 4 (over x, core), col: 8 (over z, y).
Axes of the slice: x: 2, y: 2, z: 4, core: 2. Of those that a mesh axis runs over, the one named last changes fastest.
Arguments:
- points: bfloat16 [12, 4, 512, 64], P(None, 'row', 'col'), may hold values from -7.5 to 7.5
- inverse_factor: bfloat16 [512, 512], replicated, as said below
- panel_index: int32 [1], replicated, may hold values from 3 to 23
- column_map: int32 [8], P('col'), may hold values from 0 to 7, each once
Outputs:
- panel: bfloat16 [6, 4, 512, 512], P(None, 'row', 'col')
- update: bfloat16 [6, 4, 512, 8, 512], P(None, 'row', None, 'col')
Inputs may be any that keep to these rules, and one draw needn't show every extreme that they name: `column_map`: a permutation of 0 .. 8 - 1. `inverse_factor`: zero above the diagonal.
All inputs are finite; a program needn't handle non-finite values.
Results may differ from a plain program's by a relative error of at most 0.0049.
Values may be sent and summed in bfloat16 or wider, within the bound.
No kernel may reach another device: no remote copies, remote signals or barrier semaphores. Data moves between devices by JAX's collectives and lax.ppermute only.
A program may use at most 64 MiB of HBM per device.

v0:
```python
import jax
import jax.numpy as jnp
from jax import lax
from jax.sharding import PartitionSpec as P

RW = 6
JITTER = 1.0


def kernel_tile(left_points, right_points):
    left_vals = left_points.astype(jnp.float32)
    right_vals = right_points.astype(jnp.float32)
    inner_products = lax.dot_general(
        left_points, right_points, (((1,), (1,)), ((), ())), preferred_element_type=jnp.float32
    )
    left_norms = jnp.sum(left_vals * left_vals, axis=1)
    right_norms = jnp.sum(right_vals * right_vals, axis=1)
    distance = left_norms[:, None] + right_norms[None, :] - 2.0 * inner_products
    return jnp.exp(-distance / (2.0 * left_points.shape[1]))


def panel_tile(row_points, panel_points, inverse_factor):
    rounded = kernel_tile(row_points, panel_points).astype(jnp.bfloat16)
    product = lax.dot_general(
        rounded, inverse_factor, (((1,), (1,)), ((), ())), preferred_element_type=jnp.float32
    )
    return product.astype(jnp.bfloat16)


def masked(values, keep):
    return jnp.where(keep, values.astype(jnp.float32), 0.0)


def shards(points, inverse_factor, panel_index, column_map):
    row_count = lax.axis_size("row")
    row_here = lax.axis_index("row")
    col_here = lax.axis_index("col")
    pivot_tile = panel_index[0]
    start_slot = (pivot_tile + row_count - row_here) // row_count
    local_points = lax.dynamic_slice_in_dim(points[:, 0], start_slot - 1, RW + 1, 0)
    blocks = lax.all_gather(local_points, "col", axis=1, tiled=True)
    holds_panel = row_here == pivot_tile % row_count
    panel_points = lax.psum(masked(blocks[0], holds_panel).astype(jnp.bfloat16), "row")
    window_points = blocks[1:]
    panel_full = jnp.stack(
        [
            panel_tile(window_points[window_slot], panel_points, inverse_factor)
            for window_slot in range(RW)
        ]
    )
    share_rows = local_points.shape[1]
    panel_part = lax.dynamic_slice_in_dim(panel_full, col_here * share_rows, share_rows, 1)
    column_tile = pivot_tile + 1 + column_map[0]
    holds_column = row_here == column_tile % row_count
    position = jnp.clip(column_tile // row_count - start_slot, 0, RW - 1)
    candidate_points = lax.dynamic_index_in_dim(window_points, position, 0, keepdims=False)
    candidate_rows = lax.dynamic_index_in_dim(panel_full, position, 0, keepdims=False)
    summed_points, summed_rows = (
        lax.psum(masked(candidate_points, holds_column).astype(jnp.bfloat16), "row").astype(
            jnp.float32
        ),
        lax.psum(masked(candidate_rows, holds_column).astype(jnp.bfloat16), "row").astype(
            jnp.float32
        ),
    )
    column_points = summed_points.astype(jnp.bfloat16)
    column_rows = summed_rows.astype(jnp.bfloat16)
    identity = jnp.eye(inverse_factor.shape[0], dtype=jnp.float32)
    updates = []
    for window_slot in range(RW):
        tile_row = (start_slot + window_slot) * row_count + row_here
        update_tile = kernel_tile(window_points[window_slot], column_points)
        update_tile = update_tile + jnp.where(tile_row == column_tile, JITTER, 0.0) * identity
        update_tile = update_tile - lax.dot_general(
            panel_full[window_slot],
            column_rows,
            (((1,), (1,)), ((), ())),
            preferred_element_type=jnp.float32,
        )
        updates.append(update_tile.astype(jnp.bfloat16))
    update = jnp.stack(updates)[:, None, :, None, :]
    return (panel_part[:, None], update)


def solution(mesh):
    in_specs = (P(None, "row", "col", None), P(), P(), P("col"))
    out_specs = (P(None, "row", "col", None), P(None, "row", None, "col", None))
    return jax.shard_map(shards, mesh=mesh, in_specs=in_specs, out_specs=out_specs, check_vma=False)
```

profile of v0, /device:TPU:0, one launch (start us, length us, event | category | flops | bytes accessed | tf_op | source)
XLA Modules:
  0.0 141.9 jit_solution(7604250753707338826)
XLA Ops:
  8.0 0.9 constant_dynamic-slice_fusion
  8.9 34.2 %all-gather = bf16[7,1,512,64]{3,2,1,0:T(8,128)(2,1)S(1)} all-gather(bf16[7,1,64,64]{3,2,1,0:T(8,128)(2,1)S(1)} %constant_dynamic-slice_fusion), channel_id=2, replica_groups=mesh['row'=4,'col'=8] {'col'}, dimensions={2}, use_global_device_ids=true | all-gather | bytes 516096 | tf_op jit(solution)/shard_map/all_gather | solution.py:41
  43.1 0.7 fusion.109
  43.9 0.5 multiply_reduce_fusion.1
  45.1 0.7 fusion.110
  45.8 30.7 %all-reduce.4.cloned.1.call-done = bf16[512,64]{1,0:T(8,128)(2,1)} async-done(((bf16[512,64]{1,0:T(8,128)(2,1)}), bf16[512,64]{1,0:T(8,128)(2,1)}) %all-reduce.4.cloned.1.call-update) | async-done | bytes 65552 | tf_op jit(solution)/shard_map/psum | solution.py:43
  76.6 1.1 multiply_reduce_fusion.6
  77.7 2.5 %bitcast_dynamic-update-slice_fusion.5 = (bf16[6,512,512]{2,1,0:T(8,128)(2,1)}, bf16[512,512]{1,0:T(8,128)(2,1)}) fusion(bf16[512,512]{1,0:T(8,128)(2,1)S(1)} %copy-done, bf16[512,64]{1,0:T(8,128)(2,1)} %all-reduce.4.cloned.1.call-done, f32[512]{0:T(512)S(1)} %multiply_reduce_fusion.6, f32[512]{0:T(512)S(1)} %get-tuple-element.9, ...), kind=kOutput, calls=%fused_computation.116 | convolution fusion | flops 303824896 | bytes 1773568 | tf_op jit(solution)/shard_map/dot_general | solution.py:24
  80.2 1.6 %bitcast_dynamic-update-slice_fusion.4 = (bf16[6,512,512]{2,1,0:T(8,128)(2,1)}, bf16[512,512]{1,0:T(8,128)(2,1)}) fusion(bf16[6,512,512]{2,1,0:T(8,128)(2,1)} %get-tuple-element.12, bf16[512,512]{1,0:T(8,128)(2,1)S(1)} %copy-done, bf16[512,64]{1,0:T(8,128)(2,1)S(1)} %copy-done.5, f32[512]{0:T(512)S(1)} %get-tuple-element.8, ...), kind=kOutput, calls=%fused_computation.115 | convolution fusion | flops 303824896 | bytes 1839104 | tf_op jit(solution)/shard_map/dot_general | solution.py:24
  81.9 1.4 %bitcast_dynamic-update-slice_fusion.3 = (bf16[6,512,512]{2,1,0:T(8,128)(2,1)}, bf16[512,512]{1,0:T(8,128)(2,1)S(1)}) fusion(bf16[6,512,512]{2,1,0:T(8,128)(2,1)} %get-tuple-element.14, bf16[512,512]{1,0:T(8,128)(2,1)S(1)} %copy-done, bf16[512,64]{1,0:T(8,128)(2,1)S(1)} %copy-done.5, f32[512]{0:T(512)S(1)} %get-tuple-element.7, ...), kind=kOutput, calls=%fused_computation.114 | convolution fusion | flops 303824896 | bytes 1839104 | tf_op jit(solution)/shard_map/dot_general | solution.py:24
  83.3 1.4 %bitcast_dynamic-update-slice_fusion.2 = (bf16[6,512,512]{2,1,0:T(8,128)(2,1)}, bf16[512,512]{1,0:T(8,128)(2,1)S(1)}) fusion(bf16[6,512,512]{2,1,0:T(8,128)(2,1)} %get-tuple-element.16, bf16[512,512]{1,0:T(8,128)(2,1)S(1)} %copy-done, bf16[512,64]{1,0:T(8,128)(2,1)S(1)} %copy-done.5, f32[512]{0:T(512)S(1)} %get-tuple-element.6, ...), kind=kOutput, calls=%fused_computation.113 | convolution fusion | flops 303824896 | bytes 1839104 | tf_op jit(solution)/shard_map/dot_general | solution.py:24
  84.8 1.4 %bitcast_dynamic-update-slice_fusion.1 = (bf16[6,512,512]{2,1,0:T(8,128)(2,1)}, bf16[512,512]{1,0:T(8,128)(2,1)S(1)}) fusion(bf16[6,512,512]{2,1,0:T(8,128)(2,1)} %get-tuple-element.18, bf16[512,512]{1,0:T(8,128)(2,1)S(1)} %copy-done, bf16[512,64]{1,0:T(8,128)(2,1)S(1)} %copy-done.5, f32[512]{0:T(512)S(1)} %get-tuple-element.5, ...), kind=kOutput, calls=%fused_computation.112 | convolution fusion | flops 303824896 | bytes 1839104 | tf_op jit(solution)/shard_map/dot_general | solution.py:24
  86.2 2.3 %bitcast_dynamic-update-slice_fusion = (bf16[6,512,512]{2,1,0:T(8,128)(2,1)}, bf16[512,512]{1,0:T(8,128)(2,1)S(1)}) fusion(bf16[6,512,512]{2,1,0:T(8,128)(2,1)} %get-tuple-element.20, bf16[512,512]{1,0:T(8,128)(2,1)S(1)} %copy-done, bf16[512,64]{1,0:T(8,128)(2,1)} %all-reduce.4.cloned.1.call-done, f32[512]{0:T(512)S(1)} %get-tuple-element.4, ...), kind=kOutput, calls=%fused_computation.111 | convolution fusion | flops 303824896 | bytes 1839104 | tf_op jit(solution)/shard_map/dot_general | solution.py:24
  88.5 1.9 %fusion.84 = bf16[512,512]{1,0:T(8,128)(2,1)} fusion(bf16[6,512,512]{2,1,0:T(8,128)(2,1)} %get-tuple-element.22, s32[]{:T(128)S(6)} %min.4, pred[]{:T(512)S(6)} %eq.41), kind=kLoop, calls=%fused_computation.110 | loop fusion | flops 786432 | bytes 1048581 | tf_op jit(solution)/shard_map/convert_element_type | solution.py:62
  90.6 1.8 %dynamic-slice_bitcast_fusion = bf16[6,1,64,512]{3,2,1,0:T(8,128)(2,1)} fusion(bf16[6,512,512]{2,1,0:T(8,128)(2,1)} %get-tuple-element.22, s32[]{:T(128)S(6)} %select_n.77), kind=kLoop, calls=%fused_computation.141 | loop fusion | bytes 786436 | tf_op jit(solution)/shard_map/broadcast_in_dim | solution.py:82
  92.3 32.4 %all-reduce.6.cloned.1.call-done = (bf16[512,64]{1,0:T(8,128)(2,1)}, bf16[512,512]{1,0:T(8,128)(2,1)}) async-done(((bf16[512,64]{1,0:T(8,128)(2,1)}, bf16[512,512]{1,0:T(8,128)(2,1)}), (bf16[512,64]{1,0:T(8,128)(2,1)}, bf16[512,512]{1,0:T(8,128)(2,1)})) %all-reduce.6.cloned.1.call-update) | async-done | bytes 589840 | tf_op jit(solution)/shard_map/psum | solution.py:59
  124.8 1.1 multiply_reduce_fusion
  125.9 1.3 fusion.28
  127.2 1.3 fusion.33
  128.5 0.4 fusion.38
  128.9 0.4 fusion.43
  129.4 0.4 fusion.48
  129.8 0.4 fusion.53
  130.2 0.2 copy-done.1
  130.4 0.2 copy-done.3
  130.6 0.5 fusion.77
  131.0 0.5 fusion.75
  131.5 0.5 fusion.73
  132.0 0.5 fusion.71
  132.5 0.5 fusion.69
  133.0 0.5 fusion.67
  133.4 1.7 %copy-done.6 = bf16[6,512,512]{2,1,0:T(8,128)(2,1)} copy-done((bf16[6,512,512]{2,1,0:T(8,128)(2,1)}, bf16[6,512,512]{2,1,0:T(8,128)(2,1)S(1)}, u32[]{:S(2)}) %copy-start.6) | copy-done | bytes 3145752
  (22 shorter events, 0.2 us)
Async XLA Ops:
  7.2 70.5 %copy-start = (bf16[512,512]{1,0:T(8,128)(2,1)S(1)}, bf16[512,512]{1,0:T(8,128)(2,1)}, u32[]{:S(2)}) copy-start(bf16[512,512]{1,0:T(8,128)(2,1)} %param.5) | copy-start | bytes 1572868
  7.2 69.4 %all-reduce.4.cloned.1.call-start = ((), (), s32[]{:S(2)}) async-start(), calls=%async_computation | async-start | bytes 262144 | tf_op jit(solution)/shard_map/psum | solution.py:43
  43.8 80.9 %all-reduce.6.cloned.1.call-start = ((), (), s32[]{:S(2)}) async-start(), calls=%async_computation.1 | async-start | bytes 1310720 | tf_op jit(solution)/shard_map/psum | solution.py:59
  44.4 37.5 %copy-start.7 = (f32[512]{0:T(512)}, f32[512]{0:T(512)S(1)}, u32[]{:S(2)}) copy-start(f32[512]{0:T(512)S(1)} %get-tuple-element.8) | copy-start | bytes 6148
  44.4 37.5 %copy-start.8 = (f32[512]{0:T(512)}, f32[512]{0:T(512)S(1)}, u32[]{:S(2)}) copy-start(f32[512]{0:T(512)S(1)} %get-tuple-element.9) | copy-start | bytes 6148
  76.6 3.7 %copy-start.5 = (bf16[512,64]{1,0:T(8,128)(2,1)S(1)}, bf16[512,64]{1,0:T(8,128)(2,1)}, u32[]{:S(2)}) copy-start(bf16[512,64]{1,0:T(8,128)(2,1)} %all-reduce.4.cloned.1.call-done) | copy-start | bytes 196612
  77.7 7.1 %copy-start.9 = (f32[512]{0:T(512)}, f32[512]{0:T(512)S(1)}, u32[]{:S(2)}) copy-start(f32[512]{0:T(512)S(1)} %multiply_reduce_fusion.6) | copy-start | bytes 6148
  124.8 3.8 %copy-start.4 = (bf16[512,64]{1,0:T(8,128)(2,1)S(1)}, bf16[512,64]{1,0:T(8,128)(2,1)}, u32[]{:S(2)}) copy-start(bf16[512,64]{1,0:T(8,128)(2,1)} %get-tuple-element.10) | copy-start | bytes 196612
  129.4 1.0 copy-start.1
  129.4 1.2 copy-start.3
  129.8 1.3 copy-start.2
  133.4 1.7 %copy-start.6 = (bf16[6,512,512]{2,1,0:T(8,128)(2,1)}, bf16[6,512,512]{2,1,0:T(8,128)(2,1)S(1)}, u32[]{:S(2)}) copy-start(bf16[6,512,512]{2,1,0:T(8,128)(2,1)S(1)} %fusion.67) | copy-start | bytes 9437188
Sparse Core Ops, SparseCore 0:
  43.9 32.5 all-reduce.3
  90.6 34.0 all-reduce.5
where the time goes:
time: 142 us
  waiting for transfers between devices  63.2 us (45%)
  blocking collectives  34.2 us (24%)
  matrix products  17.8 us (13%)
  between operations  15.7 us (11%)
  other arithmetic  6.04 us (4%)
  local copies, waits for them, and re-layouts  4.81 us (3%)
    all_gather x1, blocking collectives, shards(): blocks = lax.all_gather(local_points, 'col', axis=1, tiled=True)  34.2 us
    psum x1, waiting for transfers between devices, shards(): lax.psum(masked(candidate_points, holds_column).astype(jnp.bfloat16), 'row')  32.4 us
    psum x1, waiting for transfers between devices, shards(): lax.psum(masked(blocks[0], holds_panel).astype(jnp.bfloat16), 'row')  30.7 us
    dot_general x6, matrix products, panel_tile(): lax.dot_general(rounded, inverse_factor, (((1,), (1,)), ((), ())), prefer...  10.8 us
    dot_general x6, matrix products, kernel_tile(): lax.dot_general(left_points, right_points, (((1,), (1,)), ((), ())), pref...  4.21 us
  transfers between devices with their start and end apart: 2, of which 2 were waited for; matrix products, arithmetic and copies ran while one was open for 2% of the time, Pallas kernels for 0%

commit v1 on v0

--- a/solution.py
+++ b/solution.py
@@ -38,7 +38,21 @@
     pivot_tile = panel_index[0]
     start_slot = (pivot_tile + row_count - row_here) // row_count
     local_points = lax.dynamic_slice_in_dim(points[:, 0], start_slot - 1, RW + 1, 0)
-    blocks = lax.all_gather(local_points, "col", axis=1, tiled=True)
+    ways, here, turn = (lax.axis_size("col"), lax.axis_index("col"), local_points.shape[1])
+    shape = [n * ways if d == 1 else n for d, n in enumerate(local_points.shape)]
+    full = lax.dynamic_update_slice_in_dim(
+        jnp.zeros(shape, local_points.dtype), local_points, here * turn, axis=1
+    )
+    going_up = going_down = local_points
+    for far in range(1, ways // 2 + 1):
+        going_up = lax.ppermute(going_up, "col", [(d, (d + 1) % ways) for d in range(ways)])
+        full = lax.dynamic_update_slice_in_dim(full, going_up, (here - far) % ways * turn, axis=1)
+        if 2 * far < ways:
+            going_down = lax.ppermute(going_down, "col", [(d, (d - 1) % ways) for d in range(ways)])
+            full = lax.dynamic_update_slice_in_dim(
+                full, going_down, (here + far) % ways * turn, axis=1
+            )
+    blocks = full
     holds_panel = row_here == pivot_tile % row_count
     panel_points = lax.psum(masked(blocks[0], holds_panel).astype(jnp.bfloat16), "row")
     window_points = blocks[1:]

time: 142 us -> 137 us (0.965)
  blocking collectives: 34.2 us -> 0 us
  starting transfers between devices: 0.08 us -> 15.6 us
  waiting for transfers between devices: 63.2 us -> 76.5 us
    all_gather x1 -> x0, blocking collectives: 34.2 us -> none  [shards(): blocks = lax.all_gather(local_points, 'col', axis=1, tiled=True)]
    ppermute x0 -> x7, waiting for transfers between devices: none -> 15.5 us  [the longest x4 15.4 us: shards(): lax.ppermute(going_up, 'col', [(d, (d + 1) % ways) for d in range(ways)])]
    ppermute x0 -> x7, starting transfers between devices: none -> 15.5 us  [the longest x3 11 us: shards(): lax.ppermute(going_down, 'col', [(d, (d - 1) % ways) for d in range(ways)])]
    psum x1, waiting for transfers between devices: 30.7 us -> 28.5 us  [shards(): lax.psum(masked(blocks[0], holds_panel).astype(jnp.bfloat16), 'row')]
  transfers between devices with their start and end apart: 2 -> 9, of which waited for: 2 -> 7; matrix products, arithmetic and copies ran while one was open for 2% -> 2% of each run, Pallas kernels for 0% -> 0%
where the time goes in v1:
time: 137 us
  waiting for transfers between devices  76.5 us (56%)
  matrix products  17.9 us (13%)
  between operations  15.8 us (12%)
  starting transfers between devices  15.6 us (11%)
  other arithmetic  6.02 us (4%)
  local copies, waits for them, and re-layouts  5.11 us (4%)
    psum x1, waiting for transfers between devices, shards(): lax.psum(masked(candidate_points, holds_column).astype(jnp.bfloat16), 'row')  32.4 us
    psum x1, waiting for transfers between devices, shards(): lax.psum(masked(blocks[0], holds_panel).astype(jnp.bfloat16), 'row')  28.5 us
    ppermute x4, waiting for transfers between devices, shards(): lax.ppermute(going_up, 'col', [(d, (d + 1) % ways) for d in range(ways)])  15.4 us
    ppermute x3, starting transfers between devices, shards(): lax.ppermute(going_down, 'col', [(d, (d - 1) % ways) for d in range(ways)])  11 us
    dot_general x6, matrix products, panel_tile(): lax.dot_general(rounded, inverse_factor, (((1,), (1,)), ((), ())), prefer...  10.8 us
    ppermute x4, starting transfers between devices, shards(): lax.ppermute(going_up, 'col', [(d, (d + 1) % ways) for d in range(ways)])  4.55 us
    dot_general x6, matrix products, kernel_tile(): lax.dot_general(left_points, right_points, (((1,), (1,)), ((), ())), pref...  4.21 us
    dot_general x6, matrix products, shards(): lax.dot_general(panel_full[window_slot], column_rows, (((1,), (1,)), ((),...  2.82 us
  transfers between devices with their start and end apart: 9, of which 7 were waited for; matrix products, arithmetic and copies ran while one was open for 2% of the time, Pallas kernels for 0%

profile of v1, /device:TPU:0, one launch (start us, length us, event | category | flops | bytes accessed | tf_op | source)
XLA Modules:
  0.0 136.8 jit_solution(17269180298486854155)
XLA Ops:
  8.1 1.0 constant_dynamic-update-slice_fusion.7
  9.0 3.0 %collective-permute-start = (bf16[7,64,64]{2,1,0:T(8,128)(2,1)S(1)}, bf16[7,64,64]{2,1,0:T(8,128)(2,1)S(1)}, u32[]{:S(2)}, u32[]{:S(2)}) collective-permute-start(bf16[7,64,64]{2,1,0:T(8,128)(2,1)S(1)} %get-tuple-element.13), channel_id=1, source_target_pairs={{0,1},{1,2},{2,3},{3,4},{4,5},{5,6},{6,7},{7,0},{8,9},{9,10},{10,1... | collective-permute-start | bytes 172040 | tf_op jit(solution)/shard_map/ppermute | solution.py:48
  12.1 3.1 %collective-permute-start.1 = (bf16[7,64,64]{2,1,0:T(8,128)(2,1)S(1)}, bf16[7,64,64]{2,1,0:T(8,128)(2,1)S(1)}, u32[]{:S(2)}, u32[]{:S(2)}) collective-permute-start(bf16[7,64,64]{2,1,0:T(8,128)(2,1)S(1)} %get-tuple-element.13), channel_id=1, source_target_pairs={{0,7},{1,0},{2,1},{3,2},{4,3},{5,4},{6,5},{7,6},{8,15},{9,8},{10,9... | collective-permute-start | bytes 172040 | tf_op jit(solution)/shard_map/ppermute | solution.py:51
  15.9 2.5 %collective-permute-done = bf16[7,64,64]{2,1,0:T(8,128)(2,1)S(1)} collective-permute-done((bf16[7,64,64]{2,1,0:T(8,128)(2,1)S(1)}, bf16[7,64,64]{2,1,0:T(8,128)(2,1)S(1)}, u32[]{:S(2)}, u32[]{:S(2)}) %collective-permute-start) | collective-permute-done | bytes 57376 | tf_op jit(solution)/shard_map/ppermute | solution.py:48
  18.4 1.1 collective-permute-start.2
  19.4 3.7 %collective-permute-start.3 = (bf16[7,64,64]{2,1,0:T(8,128)(2,1)S(1)}, bf16[7,64,64]{2,1,0:T(8,128)(2,1)S(1)}, u32[]{:S(2)}, u32[]{:S(2)}) collective-permute-start(bf16[7,64,64]{2,1,0:T(8,128)(2,1)S(1)} %collective-permute-done.1), channel_id=1, source_target_pairs={{0,7},{1,0},{2,1},{3,2},{4,3},{5,4},{6,5},{7,6},{8,15},{9,8},{10,9... | collective-permute-start | bytes 172040 | tf_op jit(solution)/shard_map/ppermute | solution.py:51
  23.2 2.8 %collective-permute-done.2 = bf16[7,64,64]{2,1,0:T(8,128)(2,1)S(1)} collective-permute-done((bf16[7,64,64]{2,1,0:T(8,128)(2,1)S(1)}, bf16[7,64,64]{2,1,0:T(8,128)(2,1)S(1)}, u32[]{:S(2)}, u32[]{:S(2)}) %collective-permute-start.2) | collective-permute-done | bytes 57376 | tf_op jit(solution)/shard_map/ppermute | solution.py:48
  26.5 4.2 %collective-permute-start.5 = (bf16[7,64,64]{2,1,0:T(8,128)(2,1)S(1)}, bf16[7,64,64]{2,1,0:T(8,128)(2,1)S(1)}, u32[]{:S(2)}, u32[]{:S(2)}) collective-permute-start(bf16[7,64,64]{2,1,0:T(8,128)(2,1)S(1)} %collective-permute-done.3), channel_id=1, source_target_pairs={{0,7},{1,0},{2,1},{3,2},{4,3},{5,4},{6,5},{7,6},{8,15},{9,8},{10,9... | collective-permute-start | bytes 172040 | tf_op jit(solution)/shard_map/ppermute | solution.py:51
  30.7 2.7 %collective-permute-done.4 = bf16[7,64,64]{2,1,0:T(8,128)(2,1)S(1)} collective-permute-done((bf16[7,64,64]{2,1,0:T(8,128)(2,1)S(1)}, bf16[7,64,64]{2,1,0:T(8,128)(2,1)S(1)}, u32[]{:S(2)}, u32[]{:S(2)}) %collective-permute-start.4) | collective-permute-done | bytes 57376 | tf_op jit(solution)/shard_map/ppermute | solution.py:48
  33.5 7.4 %collective-permute-done.6 = bf16[7,64,64]{2,1,0:T(8,128)(2,1)S(1)} collective-permute-done((bf16[7,64,64]{2,1,0:T(8,128)(2,1)S(1)}, bf16[7,64,64]{2,1,0:T(8,128)(2,1)S(1)}, u32[]{:S(2)}, u32[]{:S(2)}) %collective-permute-start.6) | collective-permute-done | bytes 57376 | tf_op jit(solution)/shard_map/ppermute | solution.py:48
  41.0 0.5 multiply_reduce_fusion.1
  41.5 0.7 fusion.109
  42.3 0.7 fusion.110
  43.0 28.5 %all-reduce.4.cloned.1.call-done = bf16[512,64]{1,0:T(8,128)(2,1)} async-done(((bf16[512,64]{1,0:T(8,128)(2,1)}), bf16[512,64]{1,0:T(8,128)(2,1)}) %all-reduce.4.cloned.1.call-update) | async-done | bytes 65552 | tf_op jit(solution)/shard_map/psum | solution.py:57
  71.5 1.1 multiply_reduce_fusion.6
  72.6 2.5 %bitcast_dynamic-update-slice_fusion.5 = (bf16[6,512,512]{2,1,0:T(8,128)(2,1)}, bf16[512,512]{1,0:T(8,128)(2,1)}) fusion(bf16[512,512]{1,0:T(8,128)(2,1)S(1)} %copy-done, bf16[512,64]{1,0:T(8,128)(2,1)} %all-reduce.4.cloned.1.call-done, f32[512]{0:T(512)S(1)} %multiply_reduce_fusion.6, f32[512]{0:T(512)S(1)} %get-tuple-element.9, ...), kind=kOutput, calls=%fused_computation.116 | convolution fusion | flops 303824896 | bytes 1773568 | tf_op jit(solution)/shard_map/dot_general | solution.py:24
  75.1 1.6 %bitcast_dynamic-update-slice_fusion.4 = (bf16[6,512,512]{2,1,0:T(8,128)(2,1)}, bf16[512,512]{1,0:T(8,128)(2,1)}) fusion(bf16[6,512,512]{2,1,0:T(8,128)(2,1)} %get-tuple-element.14, bf16[512,512]{1,0:T(8,128)(2,1)S(1)} %copy-done, bf16[512,64]{1,0:T(8,128)(2,1)S(1)} %copy-done.5, f32[512]{0:T(512)S(1)} %get-tuple-element.8, ...), kind=kOutput, calls=%fused_computation.115 | convolution fusion | flops 303824896 | bytes 1839104 | tf_op jit(solution)/shard_map/dot_general | solution.py:24
  76.8 1.4 %bitcast_dynamic-update-slice_fusion.3 = (bf16[6,512,512]{2,1,0:T(8,128)(2,1)}, bf16[512,512]{1,0:T(8,128)(2,1)S(1)}) fusion(bf16[6,512,512]{2,1,0:T(8,128)(2,1)} %get-tuple-element.16, bf16[512,512]{1,0:T(8,128)(2,1)S(1)} %copy-done, bf16[512,64]{1,0:T(8,128)(2,1)S(1)} %copy-done.5, f32[512]{0:T(512)S(1)} %get-tuple-element.7, ...), kind=kOutput, calls=%fused_computation.114 | convolution fusion | flops 303824896 | bytes 1839104 | tf_op jit(solution)/shard_map/dot_general | solution.py:24
  78.2 1.4 %bitcast_dynamic-update-slice_fusion.2 = (bf16[6,512,512]{2,1,0:T(8,128)(2,1)}, bf16[512,512]{1,0:T(8,128)(2,1)S(1)}) fusion(bf16[6,512,512]{2,1,0:T(8,128)(2,1)} %get-tuple-element.18, bf16[512,512]{1,0:T(8,128)(2,1)S(1)} %copy-done, bf16[512,64]{1,0:T(8,128)(2,1)S(1)} %copy-done.5, f32[512]{0:T(512)S(1)} %get-tuple-element.6, ...), kind=kOutput, calls=%fused_computation.113 | convolution fusion | flops 303824896 | bytes 1839104 | tf_op jit(solution)/shard_map/dot_general | solution.py:24
  79.7 1.4 %bitcast_dynamic-update-slice_fusion.1 = (bf16[6,512,512]{2,1,0:T(8,128)(2,1)}, bf16[512,512]{1,0:T(8,128)(2,1)S(1)}) fusion(bf16[6,512,512]{2,1,0:T(8,128)(2,1)} %get-tuple-element.20, bf16[512,512]{1,0:T(8,128)(2,1)S(1)} %copy-done, bf16[512,64]{1,0:T(8,128)(2,1)S(1)} %copy-done.5, f32[512]{0:T(512)S(1)} %get-tuple-element.5, ...), kind=kOutput, calls=%fused_computation.112 | convolution fusion | flops 303824896 | bytes 1839104 | tf_op jit(solution)/shard_map/dot_general | solution.py:24
  81.1 2.3 %bitcast_dynamic-update-slice_fusion = (bf16[6,512,512]{2,1,0:T(8,128)(2,1)}, bf16[512,512]{1,0:T(8,128)(2,1)S(1)}) fusion(bf16[6,512,512]{2,1,0:T(8,128)(2,1)} %get-tuple-element.22, bf16[512,512]{1,0:T(8,128)(2,1)S(1)} %copy-done, bf16[512,64]{1,0:T(8,128)(2,1)} %all-reduce.4.cloned.1.call-done, f32[512]{0:T(512)S(1)} %get-tuple-element.4, ...), kind=kOutput, calls=%fused_computation.111 | convolution fusion | flops 303824896 | bytes 1839104 | tf_op jit(solution)/shard_map/dot_general | solution.py:24
  83.4 1.9 %fusion.84 = bf16[512,512]{1,0:T(8,128)(2,1)} fusion(bf16[6,512,512]{2,1,0:T(8,128)(2,1)} %get-tuple-element.24, s32[]{:T(128)S(6)} %min.4, pred[]{:T(512)S(6)} %eq.48), kind=kLoop, calls=%fused_computation.110 | loop fusion | flops 786432 | bytes 1048581 | tf_op jit(solution)/shard_map/convert_element_type | solution.py:76
  85.4 1.8 %dynamic-slice_bitcast_fusion = bf16[6,1,64,512]{3,2,1,0:T(8,128)(2,1)} fusion(bf16[6,512,512]{2,1,0:T(8,128)(2,1)} %get-tuple-element.24, s32[]{:T(128)S(6)} %select_n.124), kind=kLoop, calls=%fused_computation.141 | loop fusion | bytes 786436 | tf_op jit(solution)/shard_map/broadcast_in_dim | solution.py:96
  87.2 32.4 %all-reduce.6.cloned.1.call-done = (bf16[512,64]{1,0:T(8,128)(2,1)}, bf16[512,512]{1,0:T(8,128)(2,1)}) async-done(((bf16[512,64]{1,0:T(8,128)(2,1)}, bf16[512,512]{1,0:T(8,128)(2,1)}), (bf16[512,64]{1,0:T(8,128)(2,1)}, bf16[512,512]{1,0:T(8,128)(2,1)})) %all-reduce.6.cloned.1.call-update) | async-done | bytes 589840 | tf_op jit(solution)/shard_map/psum | solution.py:73
  119.6 1.1 multiply_reduce_fusion
  120.8 1.3 fusion.28
  122.1 1.3 fusion.33
  125.9 0.5 fusion.75
  126.9 0.5 fusion.71
  127.3 0.5 fusion.69
  127.8 0.5 fusion.67
  128.3 1.7 %copy-done.6 = bf16[6,512,512]{2,1,0:T(8,128)(2,1)} copy-done((bf16[6,512,512]{2,1,0:T(8,128)(2,1)}, bf16[6,512,512]{2,1,0:T(8,128)(2,1)S(1)}, u32[]{:S(2)}) %copy-start.6) | copy-done | bytes 3145752
  (43 shorter events, 3.9 us)
Async XLA Ops:
  7.2 65.4 %copy-start = (bf16[512,512]{1,0:T(8,128)(2,1)S(1)}, bf16[512,512]{1,0:T(8,128)(2,1)}, u32[]{:S(2)}) copy-start(bf16[512,512]{1,0:T(8,128)(2,1)} %param.5) | copy-start | bytes 1572868
  7.2 64.3 %all-reduce.4.cloned.1.call-start = ((), (), s32[]{:S(2)}) async-start(), calls=%async_computation | async-start | bytes 262144 | tf_op jit(solution)/shard_map/psum | solution.py:57
  9.0 9.3 %collective-permute-start = (bf16[7,64,64]{2,1,0:T(8,128)(2,1)S(1)}, bf16[7,64,64]{2,1,0:T(8,128)(2,1)S(1)}, u32[]{:S(2)}, u32[]{:S(2)}) collective-permute-start(bf16[7,64,64]{2,1,0:T(8,128)(2,1)S(1)} %get-tuple-element.13), channel_id=1, source_target_pairs={{0,1},{1,2},{2,3},{3,4},{4,5},{5,6},{6,7},{7,0},{8,9},{9,10},{10,1... | collective-permute-start | bytes 172040 | tf_op jit(solution)/shard_map/ppermute | solution.py:48
  12.1 7.3 %collective-permute-start.1 = (bf16[7,64,64]{2,1,0:T(8,128)(2,1)S(1)}, bf16[7,64,64]{2,1,0:T(8,128)(2,1)S(1)}, u32[]{:S(2)}, u32[]{:S(2)}) collective-permute-start(bf16[7,64,64]{2,1,0:T(8,128)(2,1)S(1)} %get-tuple-element.13), channel_id=1, source_target_pairs={{0,7},{1,0},{2,1},{3,2},{4,3},{5,4},{6,5},{7,6},{8,15},{9,8},{10,9... | collective-permute-start | bytes 172040 | tf_op jit(solution)/shard_map/ppermute | solution.py:51
  18.4 7.6 %collective-permute-start.2 = (bf16[7,64,64]{2,1,0:T(8,128)(2,1)S(1)}, bf16[7,64,64]{2,1,0:T(8,128)(2,1)S(1)}, u32[]{:S(2)}, u32[]{:S(2)}) collective-permute-start(bf16[7,64,64]{2,1,0:T(8,128)(2,1)S(1)} %collective-permute-done), channel_id=1, source_target_pairs={{0,1},{1,2},{2,3},{3,4},{4,5},{5,6},{6,7},{7,0},{8,9},{9,10},{10,1... | collective-permute-start | bytes 172040 | tf_op jit(solution)/shard_map/ppermute | solution.py:48
  19.4 7.1 %collective-permute-start.3 = (bf16[7,64,64]{2,1,0:T(8,128)(2,1)S(1)}, bf16[7,64,64]{2,1,0:T(8,128)(2,1)S(1)}, u32[]{:S(2)}, u32[]{:S(2)}) collective-permute-start(bf16[7,64,64]{2,1,0:T(8,128)(2,1)S(1)} %collective-permute-done.1), channel_id=1, source_target_pairs={{0,7},{1,0},{2,1},{3,2},{4,3},{5,4},{6,5},{7,6},{8,15},{9,8},{10,9... | collective-permute-start | bytes 172040 | tf_op jit(solution)/shard_map/ppermute | solution.py:51
  26.0 7.5 %collective-permute-start.4 = (bf16[7,64,64]{2,1,0:T(8,128)(2,1)S(1)}, bf16[7,64,64]{2,1,0:T(8,128)(2,1)S(1)}, u32[]{:S(2)}, u32[]{:S(2)}) collective-permute-start(bf16[7,64,64]{2,1,0:T(8,128)(2,1)S(1)} %collective-permute-done.2), channel_id=1, source_target_pairs={{0,1},{1,2},{2,3},{3,4},{4,5},{5,6},{6,7},{7,0},{8,9},{9,10},{10,1... | collective-permute-start | bytes 172040 | tf_op jit(solution)/shard_map/ppermute | solution.py:48
  26.5 7.0 %collective-permute-start.5 = (bf16[7,64,64]{2,1,0:T(8,128)(2,1)S(1)}, bf16[7,64,64]{2,1,0:T(8,128)(2,1)S(1)}, u32[]{:S(2)}, u32[]{:S(2)}) collective-permute-start(bf16[7,64,64]{2,1,0:T(8,128)(2,1)S(1)} %collective-permute-done.3), channel_id=1, source_target_pairs={{0,7},{1,0},{2,1},{3,2},{4,3},{5,4},{6,5},{7,6},{8,15},{9,8},{10,9... | collective-permute-start | bytes 172040 | tf_op jit(solution)/shard_map/ppermute | solution.py:51
  33.5 7.5 %collective-permute-start.6 = (bf16[7,64,64]{2,1,0:T(8,128)(2,1)S(1)}, bf16[7,64,64]{2,1,0:T(8,128)(2,1)S(1)}, u32[]{:S(2)}, u32[]{:S(2)}) collective-permute-start(bf16[7,64,64]{2,1,0:T(8,128)(2,1)S(1)} %collective-permute-done.4), channel_id=1, source_target_pairs={{0,1},{1,2},{2,3},{3,4},{4,5},{5,6},{6,7},{7,0},{8,9},{9,10},{10,1... | collective-permute-start | bytes 172040 | tf_op jit(solution)/shard_map/ppermute | solution.py:48
  41.5 35.3 %copy-start.7 = (f32[512]{0:T(512)}, f32[512]{0:T(512)S(1)}, u32[]{:S(2)}) copy-start(f32[512]{0:T(512)S(1)} %get-tuple-element.8) | copy-start | bytes 6148
  41.5 35.3 %copy-start.8 = (f32[512]{0:T(512)}, f32[512]{0:T(512)S(1)}, u32[]{:S(2)}) copy-start(f32[512]{0:T(512)S(1)} %get-tuple-element.9) | copy-start | bytes 6148
  42.3 77.4 %all-reduce.6.cloned.1.call-start = ((), (), s32[]{:S(2)}) async-start(), calls=%async_computation.1 | async-start | bytes 1310720 | tf_op jit(solution)/shard_map/psum | solution.py:73
  71.5 3.7 %copy-start.5 = (bf16[512,64]{1,0:T(8,128)(2,1)S(1)}, bf16[512,64]{1,0:T(8,128)(2,1)}, u32[]{:S(2)}) copy-start(bf16[512,64]{1,0:T(8,128)(2,1)} %all-reduce.4.cloned.1.call-done) | copy-start | bytes 196612
  72.6 7.1 %copy-start.9 = (f32[512]{0:T(512)}, f32[512]{0:T(512)S(1)}, u32[]{:S(2)}) copy-start(f32[512]{0:T(512)S(1)} %multiply_reduce_fusion.6) | copy-start | bytes 6148
  119.6 3.8 %copy-start.4 = (bf16[512,64]{1,0:T(8,128)(2,1)S(1)}, bf16[512,64]{1,0:T(8,128)(2,1)}, u32[]{:S(2)}) copy-start(bf16[512,64]{1,0:T(8,128)(2,1)} %get-tuple-element.10) | copy-start | bytes 196612
  124.2 1.0 copy-start.1
  124.2 1.2 copy-start.3
  124.7 1.3 copy-start.2
  128.3 1.7 %copy-start.6 = (bf16[6,512,512]{2,1,0:T(8,128)(2,1)}, bf16[6,512,512]{2,1,0:T(8,128)(2,1)S(1)}, u32[]{:S(2)}) copy-start(bf16[6,512,512]{2,1,0:T(8,128)(2,1)S(1)} %fusion.67) | copy-start | bytes 9437188
Sparse Core Ops, SparseCore 0:
  42.4 29.0 all-reduce.3
  85.5 34.0 all-reduce.5
